TPU v7x, 256 devices: a whole 4x4x8 slice. The times are simulated.
256 devices in a mesh: dp: 4 (over x_hi, core), ctx: 64 (over z, y, x_lo).
Axes of the slice: x: 4 (x_hi: 2, x_lo: 2; x = x_hi * 2 + x_lo), y: 4, z: 8, core: 2. Of those that a mesh axis runs over, the one named last changes fastest.
Arguments:
- queries: bfloat16 [4, 8192, 2560], P('dp', 'ctx'), may hold values from -6 to 6
- keys: bfloat16 [4, 8192, 512], P('dp', 'ctx'), may hold values from -6 to 6
- values: bfloat16 [4, 8192, 512], P('dp', 'ctx'), may hold values from -6 to 6
- out_grad: bfloat16 [4, 8192, 2560], P('dp', 'ctx'), may hold values from -24 to 24
- layer_input: bfloat16 [4, 8192, 5120], P('dp', 'ctx'), may hold values from -16 to 16
- doc_lens: int32 [4, 16], P('dp'), may hold values from 1 to 1024, 8192 in all within a row
Outputs:
- attn_out: bfloat16 [4, 8192, 2560], P('dp', 'ctx')
- query_grad: bfloat16 [4, 8192, 2560], P('dp', 'ctx')
- key_grad: bfloat16 [4, 8192, 512], P('dp', 'ctx')
- value_grad: bfloat16 [4, 8192, 512], P('dp', 'ctx')
- weight_grad: float32 [5120, 1024], P(('dp', 'ctx'))
Inputs may be any that keep to these rules, and one draw needn't show every extreme that they name: `doc_lens`: the documents of a micro-batch lie end to end and fill its 8192 positions; in every micro-batch the longest has exactly 1024 positions.
All inputs are finite; a program needn't handle non-finite values.
Results may differ from a plain program's by a relative error of at most 0.029.
Values may be sent and summed in bfloat16 or wider, within the bound.
No kernel may reach another device: no remote copies, remote signals or barrier semaphores. Data moves between devices by JAX's collectives and lax.ppermute only.
A program may use at most 128 MiB of HBM per device.

v0:
```python
import math
import jax
import jax.numpy as jnp
from jax import lax
from jax.sharding import Mesh
from jax.sharding import PartitionSpec as P

D = 5120
HD = 128
NEGATIVE = -1e30
CTX = ("cz", "cw")


def shifted(block, distance, n_ctx):
    route = [(i - distance, i) for i in range(n_ctx) if 0 <= i - distance < n_ctx]
    return lax.ppermute(block, CTX, route)


def doc_index(lengths_row, positions):
    bounds = jnp.cumsum(lengths_row)
    return jnp.sum((positions[:, None] >= bounds[None, :]).astype(jnp.int32), axis=1)


def make_shards(n_data, n_cz, n_cw):
    n_context = n_cz * n_cw

    def shards(queries, keys, values, out_grad, layer_input, doc_lens):
        tok_rows = queries.shape[1]
        kv_width = keys.shape[2]
        heads_kv = kv_width // HD
        group = queries.shape[2] // kv_width
        inverse = 1.0 / math.sqrt(HD)
        blocks_back = min(8, n_context // 4)
        owned = D // (n_data * n_context)
        token_rows = layer_input[0].reshape(tok_rows, n_data, n_cz, n_cw, owned)
        column_share = lax.all_to_all(token_rows, "cw", split_axis=3, concat_axis=0, tiled=True)
        column_share = column_share.reshape(tok_rows * n_cw, n_data * n_cz * owned)
        own_pair = jnp.concatenate([keys[0], values[0]], axis=1)
        earlier = [shifted(own_pair, d, n_context) for d in range(blocks_back, 0, -1)]
        window_pair = jnp.concatenate(earlier + [own_pair], axis=0)
        span = window_pair.shape[0]
        key_win = window_pair[:, :kv_width].reshape(span, heads_kv, HD)
        value_win = window_pair[:, kv_width:].reshape(span, heads_kv, HD)
        device = lax.axis_index("cz") * n_cw + lax.axis_index("cw")
        query_pos = device * tok_rows + jnp.arange(tok_rows, dtype=jnp.int32)
        key_pos = (device - blocks_back) * tok_rows + jnp.arange(span, dtype=jnp.int32)
        query_ids = doc_index(doc_lens[0], query_pos)
        key_ids = doc_index(doc_lens[0], key_pos)
        allowed = (
            (key_pos[None, :] <= query_pos[:, None])
            & (key_ids[None, :] == query_ids[:, None])
            & (key_pos[None, :] >= 0)
        )
        query_blk = queries[0].reshape(tok_rows, heads_kv, group, HD)
        grad_blk = out_grad[0].reshape(tok_rows, heads_kv, group, HD)
        scores = (
            jnp.einsum("ighd,jgd->ghij", query_blk, key_win, preferred_element_type=jnp.float32)
            * inverse
        )
        scores = jnp.where(allowed[None, None], scores, NEGATIVE)
        peak = jnp.max(scores, axis=-1, keepdims=True)
        exponent = jnp.exp(scores - peak)
        probs = exponent / jnp.sum(exponent, axis=-1, keepdims=True)
        probs_half = probs.astype(jnp.bfloat16)
        output = jnp.einsum(
            "ghij,jgd->ighd", probs_half, value_win, preferred_element_type=jnp.float32
        )
        out_half = output.astype(jnp.bfloat16)
        delta = jnp.einsum("ighd,ighd->ghi", grad_blk, out_half, preferred_element_type=jnp.float32)
        prob_grad = jnp.einsum(
            "ighd,jgd->ghij", grad_blk, value_win, preferred_element_type=jnp.float32
        )
        score_grad = (probs * (prob_grad - delta[..., None])).astype(jnp.bfloat16)
        query_part = (
            jnp.einsum("ghij,jgd->ighd", score_grad, key_win, preferred_element_type=jnp.float32)
            * inverse
        ).astype(jnp.bfloat16)
        key_part = (
            jnp.einsum("ghij,ighd->jgd", score_grad, query_blk, preferred_element_type=jnp.float32)
            * inverse
        )
        value_part = jnp.einsum(
            "ghij,ighd->jgd", probs_half, grad_blk, preferred_element_type=jnp.float32
        )
        pair_grad = jnp.concatenate(
            [key_part.reshape(span, kv_width), value_part.reshape(span, kv_width)], axis=1
        )

        def block_back(distance):
            first_row = (blocks_back - distance) * tok_rows
            return pair_grad[first_row : first_row + tok_rows]

        total = block_back(0)
        for distance in range(1, blocks_back + 1):
            total = total + shifted(block_back(distance), -distance, n_context)
        pair_half = total.astype(jnp.bfloat16)
        grad_scale = 1.0 / math.sqrt(tok_rows * n_context * n_data)
        group_grad = lax.all_gather(pair_half, "cw", axis=0, tiled=True)
        batch_grad = lax.dot_general(
            column_share, group_grad, (((0,), (0,)), ((), ())), preferred_element_type=jnp.float32
        )
        weight_grad = lax.psum_scatter(
            batch_grad * grad_scale, ("dp", "cz"), scatter_dimension=0, tiled=True
        )
        attn_out = out_half.reshape(tok_rows, group * kv_width)[None]
        query_grad = query_part.reshape(tok_rows, group * kv_width)[None]
        key_grad = pair_half[:, :kv_width][None]
        value_grad = pair_half[:, kv_width:][None]
        return (attn_out, query_grad, key_grad, value_grad, weight_grad)

    return shards


def solution(mesh):
    n_data = mesh.shape["dp"]
    n_context = mesh.shape["ctx"]
    n_cw = 8 if n_context % 8 == 0 else n_context
    n_cz = n_context // n_cw
    split = Mesh(mesh.devices.reshape(n_data, n_cz, n_cw), ("dp", "cz", "cw"))
    tokens = P("dp", CTX, None)
    in_specs = (tokens, tokens, tokens, tokens, tokens, P("dp", None))
    out_specs = (tokens, tokens, tokens, tokens, P(("dp", "cz", "cw"), None))
    return jax.shard_map(
        make_shards(n_data, n_cz, n_cw),
        mesh=split,
        in_specs=in_specs,
        out_specs=out_specs,
        check_vma=False,
    )
```

profile of v0, /device:TPU:8, one launch (start us, length us, event | category | flops | bytes accessed | tf_op | source)
XLA Modules:
  0.0 592.5 jit_solution(1896691711848036301)
XLA Ops:
  9.4 3.4 collective-permute-start.7
  12.8 3.5 collective-permute-start.6
  16.3 3.7 collective-permute-start.2
  20.0 5.9 collective-permute-start.1
  25.9 4.5 collective-permute-start
  31.5 1.9 and_and_fusion
  37.0 9.2 %collective-permute-start.3 = (bf16[128,1024]{0,1:T(8,128)(2,1)S(1)}, bf16[128,1024]{0,1:T(8,128)(2,1)S(1)}, u32[]{:S(2)}, u32[]{:S(2)}) collective-permute-start(bf16[128,1024]{0,1:T(8,128)(2,1)S(1)} %pad_maximum_fusion.1), channel_id=1, source_target_pairs={{0,5},{1,6},{2,7},{3,8},{4,9},{5,10},{6,11},{7,12},{8,13},{9,14},{... | collective-permute-start | bytes 786440 | tf_op jit(solution)/shard_map/ppermute | solution.py:16
  48.9 7.5 %collective-permute-start.5 = (bf16[128,1024]{0,1:T(8,128)(2,1)S(1)}, bf16[128,1024]{0,1:T(8,128)(2,1)S(1)}, u32[]{:S(2)}, u32[]{:S(2)}) collective-permute-start(bf16[128,1024]{0,1:T(8,128)(2,1)S(1)} %pad_maximum_fusion.1), channel_id=1, source_target_pairs={{0,3},{1,4},{2,5},{3,6},{4,7},{5,8},{6,9},{7,10},{8,11},{9,12},{10... | collective-permute-start | bytes 786440 | tf_op jit(solution)/shard_map/ppermute | solution.py:16
  56.6 5.8 collective-permute-done.4
  64.0 6.9 %fusion.35 = (f32[4,5,128]{2,1,0:T(8,128)S(1)}, f32[4,5,128,1152]{2,3,1,0:T(8,128)}) fusion(pred[128,1152]{0,1:T(8,128)(4,1)S(1)} %copy-done.11, bf16[1152,4,128,1]{0,2,3,1:T(8,128)(2,1)S(1)} %bitcast.102, bf16[128,4,5,128]{0,3,2,1:T(8,128)(2,1)S(1)} %bitcast.105), kind=kOutput, calls=%fused_computation.79 | convolution fusion | flops 766772352 | bytes 13789184 | tf_op jit(solution)/shard_map/sub | solution.py:62
  70.9 5.9 fusion.7
  76.8 3.3 fusion.36
  80.0 2.0 copy.83
  82.1 5.2 fusion.14
  87.3 5.6 fusion.2
  92.9 3.3 fusion.8
  96.2 3.1 copy.82
  99.3 2.0 fusion.25
  101.4 1.9 collective-permute-start.8
  103.3 1.9 collective-permute-start.9
  109.3 8.8 %collective-permute-done.8 = f32[128,1024]{1,0:T(8,128)S(1)} collective-permute-done((f32[128,1024]{1,0:T(8,128)S(1)}, f32[128,1024]{1,0:T(8,128)S(1)}, u32[]{:S(2)}, u32[]{:S(2)}) %collective-permute-start.8) | collective-permute-done | bytes 524320 | tf_op jit(solution)/shard_map/ppermute | solution.py:16
  119.3 4.1 collective-permute-done.9
  124.7 9.6 %collective-permute-done.10 = f32[128,1024]{1,0:T(8,128)S(1)} collective-permute-done((f32[128,1024]{1,0:T(8,128)S(1)}, f32[128,1024]{1,0:T(8,128)S(1)}, u32[]{:S(2)}, u32[]{:S(2)}) %collective-permute-start.10) | collective-permute-done | bytes 524320 | tf_op jit(solution)/shard_map/ppermute | solution.py:16
  135.6 19.8 %collective-permute-done.11 = f32[128,1024]{1,0:T(8,128)S(1)} collective-permute-done((f32[128,1024]{1,0:T(8,128)S(1)}, f32[128,1024]{1,0:T(8,128)S(1)}, u32[]{:S(2)}, u32[]{:S(2)}) %collective-permute-start.11) | collective-permute-done | bytes 524320 | tf_op jit(solution)/shard_map/ppermute | solution.py:16
  155.4 43.6 %collective-permute-done.13 = f32[128,1024]{1,0:T(8,128)S(1)} collective-permute-done((f32[128,1024]{1,0:T(8,128)S(1)}, f32[128,1024]{1,0:T(8,128)S(1)}, u32[]{:S(2)}, u32[]{:S(2)}) %collective-permute-start.13) | collective-permute-done | bytes 524320 | tf_op jit(solution)/shard_map/ppermute | solution.py:16
  199.1 5.7 collective-permute-done.15
  204.7 32.7 %collective-permute-done.14 = f32[128,1024]{1,0:T(8,128)S(1)} collective-permute-done((f32[128,1024]{1,0:T(8,128)S(1)}, f32[128,1024]{1,0:T(8,128)S(1)}, u32[]{:S(2)}, u32[]{:S(2)}) %collective-permute-start.14) | collective-permute-done | bytes 524320 | tf_op jit(solution)/shard_map/ppermute | solution.py:16
  242.2 28.6 %all_to_all.15 = bf16[128,4,8,8,20]{0,2,4,1,3:T(8,128)(2,1)S(1)} all-to-all(bf16[128,4,8,8,20]{0,2,4,1,3:T(8,128)(2,1)S(1)} %copy.85), channel_id=1, replica_groups=mesh['dp'=4,'cz'=8,'cw'=8] {'cw'}, dimensions={3} | all-to-all | bytes 2621440 | tf_op jit(solution)/shard_map/all_to_all | solution.py:36
  271.7 27.9 %all-gather.2.cloned.1.call-done = bf16[1024,1024]{1,0:T(8,128)(2,1)} async-done(((bf16[128,1024]{1,0:T(8,128)(2,1)}), bf16[1024,1024]{1,0:T(8,128)(2,1)}) %all-gather.2.cloned.1.call-update) | async-done | bytes 2097168 | tf_op jit(solution)/shard_map/all_gather | solution.py:98
  299.6 5.0 multiply_bitcast_fusion
  306.5 3.9 fusion.11
  313.4 270.1 %all-reduce.3.cloned.1.call-done = f32[640,1024]{0,1:T(8,128)} async-done(((f32[640,1024]{0,1:T(8,128)}), f32[640,1024]{0,1:T(8,128)}) %all-reduce.3.cloned.1.call-update) | async-done | bytes 2621456
  (79 shorter events, 31.0 us)
Async XLA Ops:
  7.2 27.7 %copy-start.10 = (bf16[1,128,2560]{2,1,0:T(8,128)(2,1)S(1)}, bf16[1,128,2560]{2,1,0:T(8,128)(2,1)}, u32[]{:S(2)}) copy-start(bf16[1,128,2560]{2,1,0:T(8,128)(2,1)} %param.6) | copy-start | bytes 1966084
  7.2 292.4 %all-gather.2.cloned.1.call-start = ((), (), s32[]{:S(2)}) async-start(), calls=%async_computation.1 | async-start | bytes 2359296 | tf_op jit(solution)/shard_map/all_gather | solution.py:98
  9.4 53.2 %collective-permute-start.7 = (bf16[128,1024]{0,1:T(8,128)(2,1)S(1)}, bf16[128,1024]{0,1:T(8,128)(2,1)S(1)}, u32[]{:S(2)}, u32[]{:S(2)}) collective-permute-start(bf16[128,1024]{0,1:T(8,128)(2,1)S(1)} %pad_maximum_fusion.1), channel_id=1, source_target_pairs={{0,1},{1,2},{2,3},{3,4},{4,5},{5,6},{6,7},{7,8},{8,9},{9,10},{10,1... | collective-permute-start | bytes 786440 | tf_op jit(solution)/shard_map/ppermute | solution.py:16
  12.8 49.7 %collective-permute-start.6 = (bf16[128,1024]{0,1:T(8,128)(2,1)S(1)}, bf16[128,1024]{0,1:T(8,128)(2,1)S(1)}, u32[]{:S(2)}, u32[]{:S(2)}) collective-permute-start(bf16[128,1024]{0,1:T(8,128)(2,1)S(1)} %pad_maximum_fusion.1), channel_id=1, source_target_pairs={{0,2},{1,3},{2,4},{3,5},{4,6},{5,7},{6,8},{7,9},{8,10},{9,11},{10,... | collective-permute-start | bytes 786440 | tf_op jit(solution)/shard_map/ppermute | solution.py:16
  16.3 32.7 %collective-permute-start.2 = (bf16[128,1024]{0,1:T(8,128)(2,1)S(1)}, bf16[128,1024]{0,1:T(8,128)(2,1)S(1)}, u32[]{:S(2)}, u32[]{:S(2)}) collective-permute-start(bf16[128,1024]{0,1:T(8,128)(2,1)S(1)} %pad_maximum_fusion.1), channel_id=1, source_target_pairs={{0,6},{1,7},{2,8},{3,9},{4,10},{5,11},{6,12},{7,13},{8,14},{9,15},... | collective-permute-start | bytes 786440 | tf_op jit(solution)/shard_map/ppermute | solution.py:16
  20.0 27.2 %collective-permute-start.1 = (bf16[128,1024]{0,1:T(8,128)(2,1)S(1)}, bf16[128,1024]{0,1:T(8,128)(2,1)S(1)}, u32[]{:S(2)}, u32[]{:S(2)}) collective-permute-start(bf16[128,1024]{0,1:T(8,128)(2,1)S(1)} %pad_maximum_fusion.1), channel_id=1, source_target_pairs={{0,7},{1,8},{2,9},{3,10},{4,11},{5,12},{6,13},{7,14},{8,15},{9,16}... | collective-permute-start | bytes 786440 | tf_op jit(solution)/shard_map/ppermute | solution.py:16
  25.9 11.1 %collective-permute-start = (bf16[128,1024]{0,1:T(8,128)(2,1)S(1)}, bf16[128,1024]{0,1:T(8,128)(2,1)}, u32[]{:S(2)}, u32[]{:S(2)}) collective-permute-start(bf16[128,1024]{0,1:T(8,128)(2,1)S(1)} %pad_maximum_fusion.1), channel_id=1, source_target_pairs={{0,8},{1,9},{2,10},{3,11},{4,12},{5,13},{6,14},{7,15},{8,16},{9,17... | collective-permute-start | bytes 786440 | tf_op jit(solution)/shard_map/ppermute | solution.py:16
  35.2 28.8 %copy-start.7 = (bf16[1,128,2560]{1,2,0:T(8,128)(2,1)}, bf16[1,128,2560]{1,2,0:T(8,128)(2,1)S(1)}, u32[]{:S(2)}) copy-start(bf16[1,128,2560]{1,2,0:T(8,128)(2,1)S(1)} %copy.72) | copy-start | bytes 1966084
  37.0 19.5 %collective-permute-start.3 = (bf16[128,1024]{0,1:T(8,128)(2,1)S(1)}, bf16[128,1024]{0,1:T(8,128)(2,1)S(1)}, u32[]{:S(2)}, u32[]{:S(2)}) collective-permute-start(bf16[128,1024]{0,1:T(8,128)(2,1)S(1)} %pad_maximum_fusion.1), channel_id=1, source_target_pairs={{0,5},{1,6},{2,7},{3,8},{4,9},{5,10},{6,11},{7,12},{8,13},{9,14},{... | collective-permute-start | bytes 786440 | tf_op jit(solution)/shard_map/ppermute | solution.py:16
  47.2 15.1 %collective-permute-start.4 = (bf16[128,1024]{0,1:T(8,128)(2,1)S(1)}, bf16[128,1024]{0,1:T(8,128)(2,1)S(1)}, u32[]{:S(2)}, u32[]{:S(2)}) collective-permute-start(bf16[128,1024]{0,1:T(8,128)(2,1)S(1)} %pad_maximum_fusion.1), channel_id=1, source_target_pairs={{0,4},{1,5},{2,6},{3,7},{4,8},{5,9},{6,10},{7,11},{8,12},{9,13},{1... | collective-permute-start | bytes 786440 | tf_op jit(solution)/shard_map/ppermute | solution.py:16
  48.9 13.5 %collective-permute-start.5 = (bf16[128,1024]{0,1:T(8,128)(2,1)S(1)}, bf16[128,1024]{0,1:T(8,128)(2,1)S(1)}, u32[]{:S(2)}, u32[]{:S(2)}) collective-permute-start(bf16[128,1024]{0,1:T(8,128)(2,1)S(1)} %pad_maximum_fusion.1), channel_id=1, source_target_pairs={{0,3},{1,4},{2,5},{3,6},{4,7},{5,8},{6,9},{7,10},{8,11},{9,12},{10... | collective-permute-start | bytes 786440 | tf_op jit(solution)/shard_map/ppermute | solution.py:16
  62.7 1.3 copy-start.11
  64.0 6.9 %copy-start.4 = (bf16[1152,512]{0,1:T(8,128)(2,1)}, bf16[1152,512]{0,1:T(8,128)(2,1)S(1)}, u32[]{:S(2)}) copy-start(bf16[1152,512]{0,1:T(8,128)(2,1)S(1)} %get-tuple-element.33) | copy-start | bytes 3538948
  76.8 3.3 copy-start
  82.1 5.2 copy-start.3
  87.3 5.6 copy-start.8
  92.9 3.3 copy-start.1
  99.3 138.2 %copy-start.2 = (f32[1152,512]{1,0:T(8,128)S(1)}, f32[1152,512]{1,0:T(8,128)}, u32[]{:S(2)}) copy-start(f32[1152,512]{1,0:T(8,128)} %copy.82) | copy-start | bytes 7077892
  101.4 16.7 %collective-permute-start.8 = (f32[128,1024]{1,0:T(8,128)S(1)}, f32[128,1024]{1,0:T(8,128)S(1)}, u32[]{:S(2)}, u32[]{:S(2)}) collective-permute-start(f32[128,1024]{1,0:T(8,128)S(1)} %get-tuple-element.25), channel_id=1, source_target_pairs={{1,0},{2,1},{3,2},{4,3},{5,4},{6,5},{7,6},{8,7},{9,8},{10,9},{11,1... | collective-permute-start | bytes 1572872 | tf_op jit(solution)/shard_map/ppermute | solution.py:16
  103.3 20.1 %collective-permute-start.9 = (f32[128,1024]{1,0:T(8,128)S(1)}, f32[128,1024]{1,0:T(8,128)S(1)}, u32[]{:S(2)}, u32[]{:S(2)}) collective-permute-start(f32[128,1024]{1,0:T(8,128)S(1)} %get-tuple-element.26), channel_id=1, source_target_pairs={{2,0},{3,1},{4,2},{5,3},{6,4},{7,5},{8,6},{9,7},{10,8},{11,9},{12,... | collective-permute-start | bytes 1572872 | tf_op jit(solution)/shard_map/ppermute | solution.py:16
  105.2 29.1 %collective-permute-start.10 = (f32[128,1024]{1,0:T(8,128)S(1)}, f32[128,1024]{1,0:T(8,128)S(1)}, u32[]{:S(2)}, u32[]{:S(2)}) collective-permute-start(f32[128,1024]{1,0:T(8,128)S(1)} %get-tuple-element.27), channel_id=1, source_target_pairs={{3,0},{4,1},{5,2},{6,3},{7,4},{8,5},{9,6},{10,7},{11,8},{12,9},{13... | collective-permute-start | bytes 1572872 | tf_op jit(solution)/shard_map/ppermute | solution.py:16
  106.7 48.7 %collective-permute-start.11 = (f32[128,1024]{1,0:T(8,128)S(1)}, f32[128,1024]{1,0:T(8,128)S(1)}, u32[]{:S(2)}, u32[]{:S(2)}) collective-permute-start(f32[128,1024]{1,0:T(8,128)S(1)} %get-tuple-element.28), channel_id=1, source_target_pairs={{4,0},{5,1},{6,2},{7,3},{8,4},{9,5},{10,6},{11,7},{12,8},{13,9},{1... | collective-permute-start | bytes 1572872 | tf_op jit(solution)/shard_map/ppermute | solution.py:16
  108.0 47.4 %collective-permute-start.12 = (f32[128,1024]{1,0:T(8,128)S(1)}, f32[128,1024]{1,0:T(8,128)S(1)}, u32[]{:S(2)}, u32[]{:S(2)}) collective-permute-start(f32[128,1024]{1,0:T(8,128)S(1)} %get-tuple-element.29), channel_id=1, source_target_pairs={{5,0},{6,1},{7,2},{8,3},{9,4},{10,5},{11,6},{12,7},{13,8},{14,9},{... | collective-permute-start | bytes 1572872 | tf_op jit(solution)/shard_map/ppermute | solution.py:16
  118.0 81.0 %collective-permute-start.13 = (f32[128,1024]{1,0:T(8,128)S(1)}, f32[128,1024]{1,0:T(8,128)S(1)}, u32[]{:S(2)}, u32[]{:S(2)}) collective-permute-start(f32[128,1024]{1,0:T(8,128)S(1)} %get-tuple-element.30), channel_id=1, source_target_pairs={{6,0},{7,1},{8,2},{9,3},{10,4},{11,5},{12,6},{13,7},{14,8},{15,9},... | collective-permute-start | bytes 1572872 | tf_op jit(solution)/shard_map/ppermute | solution.py:16
  123.4 81.3 %collective-permute-start.15 = (f32[128,1024]{1,0:T(8,128)S(1)}, f32[128,1024]{1,0:T(8,128)S(1)}, u32[]{:S(2)}, u32[]{:S(2)}) collective-permute-start(f32[128,1024]{1,0:T(8,128)S(1)} %get-tuple-element.31), channel_id=1, source_target_pairs={{8,0},{9,1},{10,2},{11,3},{12,4},{13,5},{14,6},{15,7},{16,8},{17,9... | collective-permute-start | bytes 1572872 | tf_op jit(solution)/shard_map/ppermute | solution.py:16
  134.3 103.2 %collective-permute-start.14 = (f32[128,1024]{1,0:T(8,128)S(1)}, f32[128,1024]{1,0:T(8,128)S(1)}, u32[]{:S(2)}, u32[]{:S(2)}) collective-permute-start(f32[128,1024]{1,0:T(8,128)S(1)} %get-tuple-element.32), channel_id=1, source_target_pairs={{7,0},{8,1},{9,2},{10,3},{11,4},{12,5},{13,6},{14,7},{15,8},{16,9}... | collective-permute-start | bytes 1572872 | tf_op jit(solution)/shard_map/ppermute | solution.py:16
  238.6 344.8 %all-reduce.3.cloned.1.call-start = ((), (), s32[]{:S(2)}) async-start(), calls=%async_computation.2 | async-start | bytes 5242880
  304.6 0.7 copy-start.12
  304.6 1.9 copy-start.5
  306.5 5.1 copy-start.6
  310.5 2.2 copy-start.9
Sparse Core Ops, SparseCore 0:
  238.7 60.8 all-gather.1
  304.7 278.6 all-reduce.2
where the time goes:
time: 593 us
  waiting for transfers between devices  430 us (73%)
  starting transfers between devices  51.1 us (9%)
  matrix products  33.1 us (6%)
  blocking collectives  28.6 us (5%)
  local copies, waits for them, and re-layouts  23.2 us (4%)
  between operations  15.1 us (3%)
  other arithmetic  11.4 us (2%)
    unnamed x3, waiting for transfers between devices  270 us
    ppermute x16, waiting for transfers between devices, shifted(): return lax.ppermute(block, CTX, route)  132 us
    ppermute x16, starting transfers between devices, shifted(): return lax.ppermute(block, CTX, route)  51.1 us
    all_to_all x1, blocking collectives, shards(): lax.all_to_all(token_rows, 'cw', split_axis=3, concat_axis=0, tiled=True)  28.6 us
    all_gather x1, waiting for transfers between devices, shards(): group_grad = lax.all_gather(pair_half, 'cw', axis=0, tiled=True)  27.9 us
    unnamed x44, local copies, waits for them, and re-layouts  12.8 us
  transfers between devices with their start and end apart: 18, of which 11 were waited for; matrix products, arithmetic and copies ran while one was open for 3% of the time, Pallas kernels for 0%

commit v1 on v0

--- a/solution.py
+++ b/solution.py
@@ -33,7 +33,10 @@
         blocks_back = min(8, n_context // 4)
         owned = D // (n_data * n_context)
         token_rows = layer_input[0].reshape(tok_rows, n_data, n_cz, n_cw, owned)
-        column_share = lax.all_to_all(token_rows, "cw", split_axis=3, concat_axis=0, tiled=True)
+        size = lax.axis_size("cw")
+        blocks = jnp.stack(jnp.split(token_rows, size, axis=3), axis=0)
+        blocks = lax.all_to_all(blocks, "cw", split_axis=0, concat_axis=0)
+        column_share = jnp.concatenate(blocks, axis=0)
         column_share = column_share.reshape(tok_rows * n_cw, n_data * n_cz * owned)
         own_pair = jnp.concatenate([keys[0], values[0]], axis=1)
         earlier = [shifted(own_pair, d, n_context) for d in range(blocks_back, 0, -1)]

time: 593 us -> 437 us (0.74)
  waiting for transfers between devices: 430 us -> 188 us
  blocking collectives: 28.6 us -> 88 us
  starting transfers between devices: 51.1 us -> 74.8 us
    unnamed x3 -> x7, waiting for transfers between devices: 270 us -> 3.89 us
    unnamed x0 -> x1, blocking collectives: none -> 88 us
    all_to_all x1 -> x0, blocking collectives: 28.6 us -> none  [shards(): lax.all_to_all(token_rows, 'cw', split_axis=3, concat_axis=0, tiled=True)]
    all_to_all x0 -> x1, waiting for transfers between devices: none -> 24.3 us  [shards(): blocks = lax.all_to_all(blocks, 'cw', split_axis=0, concat_axis=0)]
    unnamed x1 -> x6, starting transfers between devices: 0.04 us -> 20.2 us
    unnamed x44 -> x52, local copies, waits for them, and re-layouts: 12.8 us -> 11.7 us
  transfers between devices with their start and end apart: 18 -> 24, of which waited for: 11 -> 13; matrix products, arithmetic and copies ran while one was open for 3% -> 4% of each run, Pallas kernels for 0% -> 0%
where the time goes in v1:
time: 437 us; the launch traced here: 432 us
  waiting for transfers between devices  188 us (43%)
  blocking collectives  88 us (20%)
  starting transfers between devices  74.8 us (17%)
  matrix products  32.7 us (7%)
  local copies, waits for them, and re-layouts  21.9 us (5%)
  between operations  15.3 us (4%)
  other arithmetic  11.4 us (3%)
    ppermute x16, waiting for transfers between devices, shifted(): return lax.ppermute(block, CTX, route)  132 us
    unnamed x1, blocking collectives  88 us
    ppermute x16, starting transfers between devices, shifted(): return lax.ppermute(block, CTX, route)  51.1 us
    all_gather x1, waiting for transfers between devices, shards(): group_grad = lax.all_gather(pair_half, 'cw', axis=0, tiled=True)  27.7 us
    all_to_all x1, waiting for transfers between devices, shards(): blocks = lax.all_to_all(blocks, 'cw', split_axis=0, concat_axis=0)  24.3 us
    unnamed x6, starting transfers between devices  20.2 us
    unnamed x52, local copies, waits for them, and re-layouts  11.7 us
  transfers between devices with their start and end apart: 24, of which 13 were waited for; matrix products, arithmetic and copies ran while one was open for 4% of the time, Pallas kernels for 0%

profile of v1, /device:TPU:8, one launch (start us, length us, event | category | flops | bytes accessed | tf_op | source)
XLA Modules:
  0.0 431.8 jit_solution(9384315331336903333)
XLA Ops:
  9.4 3.4 collective-permute-start.7
  12.8 3.5 collective-permute-start.6
  16.3 3.7 collective-permute-start.2
  20.0 5.9 %collective-permute-start.1 = (bf16[128,1024]{0,1:T(8,128)(2,1)S(1)}, bf16[128,1024]{0,1:T(8,128)(2,1)S(1)}, u32[]{:S(2)}, u32[]{:S(2)}) collective-permute-start(bf16[128,1024]{0,1:T(8,128)(2,1)S(1)} %pad_maximum_fusion.1), channel_id=1, source_target_pairs={{0,7},{1,8},{2,9},{3,10},{4,11},{5,12},{6,13},{7,14},{8,15},{9,16}... | collective-permute-start | bytes 786440 | tf_op jit(solution)/shard_map/ppermute | solution.py:16
  25.9 4.5 %collective-permute-start = (bf16[128,1024]{0,1:T(8,128)(2,1)S(1)}, bf16[128,1024]{0,1:T(8,128)(2,1)}, u32[]{:S(2)}, u32[]{:S(2)}) collective-permute-start(bf16[128,1024]{0,1:T(8,128)(2,1)S(1)} %pad_maximum_fusion.1), channel_id=1, source_target_pairs={{0,8},{1,9},{2,10},{3,11},{4,12},{5,13},{6,14},{7,15},{8,16},{9,17... | collective-permute-start | bytes 786440 | tf_op jit(solution)/shard_map/ppermute | solution.py:16
  37.0 9.2 %collective-permute-start.3 = (bf16[128,1024]{0,1:T(8,128)(2,1)S(1)}, bf16[128,1024]{0,1:T(8,128)(2,1)S(1)}, u32[]{:S(2)}, u32[]{:S(2)}) collective-permute-start(bf16[128,1024]{0,1:T(8,128)(2,1)S(1)} %pad_maximum_fusion.1), channel_id=1, source_target_pairs={{0,5},{1,6},{2,7},{3,8},{4,9},{5,10},{6,11},{7,12},{8,13},{9,14},{... | collective-permute-start | bytes 786440 | tf_op jit(solution)/shard_map/ppermute | solution.py:16
  48.9 7.5 %collective-permute-start.5 = (bf16[128,1024]{0,1:T(8,128)(2,1)S(1)}, bf16[128,1024]{0,1:T(8,128)(2,1)S(1)}, u32[]{:S(2)}, u32[]{:S(2)}) collective-permute-start(bf16[128,1024]{0,1:T(8,128)(2,1)S(1)} %pad_maximum_fusion.1), channel_id=1, source_target_pairs={{0,3},{1,4},{2,5},{3,6},{4,7},{5,8},{6,9},{7,10},{8,11},{9,12},{10... | collective-permute-start | bytes 786440 | tf_op jit(solution)/shard_map/ppermute | solution.py:16
  56.6 5.8 %collective-permute-done.4 = bf16[128,1024]{0,1:T(8,128)(2,1)S(1)} collective-permute-done((bf16[128,1024]{0,1:T(8,128)(2,1)S(1)}, bf16[128,1024]{0,1:T(8,128)(2,1)S(1)}, u32[]{:S(2)}, u32[]{:S(2)}) %collective-permute-start.4) | collective-permute-done | bytes 262176 | tf_op jit(solution)/shard_map/ppermute | solution.py:16
  64.0 6.9 %fusion.44 = (f32[4,5,128]{2,1,0:T(8,128)S(1)}, f32[4,5,128,1152]{2,3,1,0:T(8,128)}) fusion(pred[128,1152]{0,1:T(8,128)(4,1)S(1)} %copy-done.11, bf16[1152,4,128,1]{0,2,3,1:T(8,128)(2,1)S(1)} %bitcast.140, bf16[128,4,5,128]{0,3,2,1:T(8,128)(2,1)S(1)} %bitcast.143), kind=kOutput, calls=%fused_computation.95 | convolution fusion | flops 766772352 | bytes 13789184 | tf_op jit(solution)/shard_map/sub | solution.py:65
  70.9 5.9 %fusion.8 = bf16[4,5,128,1152]{2,3,1,0:T(8,128)(2,1)S(1)} fusion(f32[4,5,128,1152]{2,3,1,0:T(8,128)} %get-tuple-element.38, f32[4,5,128]{2,1,0:T(8,128)S(1)} %get-tuple-element.37), kind=kLoop, calls=%fused_computation.27 | loop fusion | flops 5898240 | bytes 17704960 | tf_op jit(solution)/shard_map/convert_element_type | solution.py:67
  76.8 3.3 fusion.45
  82.1 5.2 %fusion.15 = (f32[4,5,128]{2,1,0:T(8,128)S(1)}, bf16[4,128,5,128]{3,1,2,0:T(8,128)(2,1)}) fusion(bf16[4,5,128,128]{2,3,1,0:T(8,128)(2,1)S(1)} %bitcast.136, bf16[1152,4,128,1]{0,2,3,1:T(8,128)(2,1)} %bitcast.138, bf16[4,5,128,1152]{2,3,1,0:T(8,128)(2,1)} %copy-done), kind=kOutput, calls=%fused_computation.38 | convolution fusion | flops 756610560 | bytes 8398848 | tf_op jit(solution)/shard_map/ghij,jgd->ighd/dot_general | solution.py:68
  87.3 5.6 %fusion.3 = bf16[4,5,128,1152]{2,3,1,0:T(8,128)(2,1)S(1)} fusion(bf16[1152,4,128,1]{0,2,3,1:T(8,128)(2,1)S(1)} %bitcast.139, bf16[128,4,5,128]{0,3,2,1:T(8,128)(2,1)S(1)} %bitcast.137, f32[4,5,128]{2,1,0:T(8,128)S(1)} %get-tuple-element.39, f32[4,5,128,1152]{2,3,1,0:T(8,128)} %get-tuple-element.38, f32[4,5,128]{2,1,0:T(8,128)S(1)} %get-tuple-element.37), kind=kOutput, calls=%fused_computation.3 | convolution fusion | flops 766771200 | bytes 19550208 | tf_op jit(solution)/shard_map/ighd,jgd->ghij/dot_general | solution.py:73
  92.9 3.3 fusion.9
  96.2 3.1 copy.102
  109.3 8.8 %collective-permute-done.8 = f32[128,1024]{1,0:T(8,128)S(1)} collective-permute-done((f32[128,1024]{1,0:T(8,128)S(1)}, f32[128,1024]{1,0:T(8,128)S(1)}, u32[]{:S(2)}, u32[]{:S(2)}) %collective-permute-start.8) | collective-permute-done | bytes 524320 | tf_op jit(solution)/shard_map/ppermute | solution.py:16
  119.3 4.1 collective-permute-done.9
  124.7 9.6 %collective-permute-done.10 = f32[128,1024]{1,0:T(8,128)S(1)} collective-permute-done((f32[128,1024]{1,0:T(8,128)S(1)}, f32[128,1024]{1,0:T(8,128)S(1)}, u32[]{:S(2)}, u32[]{:S(2)}) %collective-permute-start.10) | collective-permute-done | bytes 524320 | tf_op jit(solution)/shard_map/ppermute | solution.py:16
  135.5 19.9 %collective-permute-done.11 = f32[128,1024]{1,0:T(8,128)S(1)} collective-permute-done((f32[128,1024]{1,0:T(8,128)S(1)}, f32[128,1024]{1,0:T(8,128)S(1)}, u32[]{:S(2)}, u32[]{:S(2)}) %collective-permute-start.11) | collective-permute-done | bytes 524320 | tf_op jit(solution)/shard_map/ppermute | solution.py:16
  155.4 43.5 %collective-permute-done.13 = f32[128,1024]{1,0:T(8,128)S(1)} collective-permute-done((f32[128,1024]{1,0:T(8,128)S(1)}, f32[128,1024]{1,0:T(8,128)S(1)}, u32[]{:S(2)}, u32[]{:S(2)}) %collective-permute-start.13) | collective-permute-done | bytes 524320 | tf_op jit(solution)/shard_map/ppermute | solution.py:16
  198.9 5.8 %collective-permute-done.15 = f32[128,1024]{1,0:T(8,128)S(1)} collective-permute-done((f32[128,1024]{1,0:T(8,128)S(1)}, f32[128,1024]{1,0:T(8,128)S(1)}, u32[]{:S(2)}, u32[]{:S(2)}) %collective-permute-start.15) | collective-permute-done | bytes 524320 | tf_op jit(solution)/shard_map/ppermute | solution.py:16
  204.7 32.7 %collective-permute-done.14 = f32[128,1024]{1,0:T(8,128)S(1)} collective-permute-done((f32[128,1024]{1,0:T(8,128)S(1)}, f32[128,1024]{1,0:T(8,128)S(1)}, u32[]{:S(2)}, u32[]{:S(2)}) %collective-permute-start.14) | collective-permute-done | bytes 524320 | tf_op jit(solution)/shard_map/ppermute | solution.py:16
  242.2 3.5 all-to-all-start
  247.0 24.3 %all-to-all-done = bf16[8,128,4,8,1,20]{1,3,5,4,2,0:T(8,128)(2,1)S(1)} async-done(((bf16[8,128,4,8,1,20]{1,3,5,4,2,0:T(8,128)(2,1)}), bf16[8,128,4,8,1,20]{1,3,5,4,2,0:T(8,128)(2,1)S(1)}, u32[]{:S(2)}, u32[]{:S(2)}) %all-to-all-start) | async-done | bytes 1310752 | tf_op jit(solution)/shard_map/all_to_all | solution.py:38
  272.1 27.7 %all-gather.2.cloned.1.call-done = bf16[1024,1024]{1,0:T(8,128)(2,1)} async-done(((bf16[128,1024]{1,0:T(8,128)(2,1)}), bf16[1024,1024]{1,0:T(8,128)(2,1)}) %all-gather.2.cloned.1.call-update) | async-done | bytes 2097168 | tf_op jit(solution)/shard_map/all_gather | solution.py:101
  299.8 4.7 %convolution_multiply_fusion = f32[640,1024]{1,0:T(8,128)} fusion(bf16[1024,1024]{1,0:T(8,128)(2,1)} %all-gather.2.cloned.1.call-done, bf16[80,8,8,128]{3,2,1,0:T(8,128)(2,1)S(1)} %bitcast.146), kind=kOutput, calls=%fused_computation.31 | convolution fusion | flops 1342832640 | bytes 6029312 | tf_op jit(solution)/shard_map/dot_general | solution.py:102
  304.4 88.0 %fusion = f32[24,1024]{1,0:T(8,128)S(1)} fusion(f32[640,1024]{1,0:T(8,128)} %convolution_multiply_fusion), kind=kCustom, calls=%all-reduce-scatter | all-reduce-scatter fusion | flops 786433 | bytes 2720768
  393.9 3.9 fusion.12
  401.3 5.2 %collective-permute-start.19 = (f32[24,1024]{1,0:T(8,128)S(1)}, f32[24,1024]{1,0:T(8,128)S(1)}, u32[]{:S(2)}, u32[]{:S(2)}) collective-permute-start(f32[24,1024]{1,0:T(8,128)S(1)} %fusion), channel_id=1, source_target_pairs={{0,32},{8,40},{16,48},{24,56},{32,64},{40,72},{48,80},{56,88},{64,... | collective-permute-start | bytes 294920
  406.5 5.1 %collective-permute-start.18 = (f32[24,1024]{1,0:T(8,128)S(1)}, f32[24,1024]{1,0:T(8,128)S(1)}, u32[]{:S(2)}, u32[]{:S(2)}) collective-permute-start(f32[24,1024]{1,0:T(8,128)S(1)} %fusion), channel_id=1, source_target_pairs={{0,24},{8,32},{16,40},{24,48},{32,56},{40,64},{48,72},{56,80},{64,... | collective-permute-start | bytes 294920
  411.6 3.8 collective-permute-start.17
  415.4 3.4 collective-permute-start.16
  (99 shorter events, 46.1 us)
Async XLA Ops:
  7.2 27.7 %copy-start.10 = (bf16[1,128,2560]{2,1,0:T(8,128)(2,1)S(1)}, bf16[1,128,2560]{2,1,0:T(8,128)(2,1)}, u32[]{:S(2)}) copy-start(bf16[1,128,2560]{2,1,0:T(8,128)(2,1)} %param.6) | copy-start | bytes 1966084
  7.2 292.6 %all-gather.2.cloned.1.call-start = ((), (), s32[]{:S(2)}) async-start(), calls=%async_computation.1 | async-start | bytes 2359296 | tf_op jit(solution)/shard_map/all_gather | solution.py:101
  9.4 53.2 %collective-permute-start.7 = (bf16[128,1024]{0,1:T(8,128)(2,1)S(1)}, bf16[128,1024]{0,1:T(8,128)(2,1)S(1)}, u32[]{:S(2)}, u32[]{:S(2)}) collective-permute-start(bf16[128,1024]{0,1:T(8,128)(2,1)S(1)} %pad_maximum_fusion.1), channel_id=1, source_target_pairs={{0,1},{1,2},{2,3},{3,4},{4,5},{5,6},{6,7},{7,8},{8,9},{9,10},{10,1... | collective-permute-start | bytes 786440 | tf_op jit(solution)/shard_map/ppermute | solution.py:16
  12.8 49.7 %collective-permute-start.6 = (bf16[128,1024]{0,1:T(8,128)(2,1)S(1)}, bf16[128,1024]{0,1:T(8,128)(2,1)S(1)}, u32[]{:S(2)}, u32[]{:S(2)}) collective-permute-start(bf16[128,1024]{0,1:T(8,128)(2,1)S(1)} %pad_maximum_fusion.1), channel_id=1, source_target_pairs={{0,2},{1,3},{2,4},{3,5},{4,6},{5,7},{6,8},{7,9},{8,10},{9,11},{10,... | collective-permute-start | bytes 786440 | tf_op jit(solution)/shard_map/ppermute | solution.py:16
  16.3 32.7 %collective-permute-start.2 = (bf16[128,1024]{0,1:T(8,128)(2,1)S(1)}, bf16[128,1024]{0,1:T(8,128)(2,1)S(1)}, u32[]{:S(2)}, u32[]{:S(2)}) collective-permute-start(bf16[128,1024]{0,1:T(8,128)(2,1)S(1)} %pad_maximum_fusion.1), channel_id=1, source_target_pairs={{0,6},{1,7},{2,8},{3,9},{4,10},{5,11},{6,12},{7,13},{8,14},{9,15},... | collective-permute-start | bytes 786440 | tf_op jit(solution)/shard_map/ppermute | solution.py:16
  20.0 27.2 %collective-permute-start.1 = (bf16[128,1024]{0,1:T(8,128)(2,1)S(1)}, bf16[128,1024]{0,1:T(8,128)(2,1)S(1)}, u32[]{:S(2)}, u32[]{:S(2)}) collective-permute-start(bf16[128,1024]{0,1:T(8,128)(2,1)S(1)} %pad_maximum_fusion.1), channel_id=1, source_target_pairs={{0,7},{1,8},{2,9},{3,10},{4,11},{5,12},{6,13},{7,14},{8,15},{9,16}... | collective-permute-start | bytes 786440 | tf_op jit(solution)/shard_map/ppermute | solution.py:16
  25.9 11.1 %collective-permute-start = (bf16[128,1024]{0,1:T(8,128)(2,1)S(1)}, bf16[128,1024]{0,1:T(8,128)(2,1)}, u32[]{:S(2)}, u32[]{:S(2)}) collective-permute-start(bf16[128,1024]{0,1:T(8,128)(2,1)S(1)} %pad_maximum_fusion.1), channel_id=1, source_target_pairs={{0,8},{1,9},{2,10},{3,11},{4,12},{5,13},{6,14},{7,15},{8,16},{9,17... | collective-permute-start | bytes 786440 | tf_op jit(solution)/shard_map/ppermute | solution.py:16
  35.2 28.8 %copy-start.7 = (bf16[1,128,2560]{1,2,0:T(8,128)(2,1)}, bf16[1,128,2560]{1,2,0:T(8,128)(2,1)S(1)}, u32[]{:S(2)}) copy-start(bf16[1,128,2560]{1,2,0:T(8,128)(2,1)S(1)} %copy.92) | copy-start | bytes 1966084
  37.0 19.5 %collective-permute-start.3 = (bf16[128,1024]{0,1:T(8,128)(2,1)S(1)}, bf16[128,1024]{0,1:T(8,128)(2,1)S(1)}, u32[]{:S(2)}, u32[]{:S(2)}) collective-permute-start(bf16[128,1024]{0,1:T(8,128)(2,1)S(1)} %pad_maximum_fusion.1), channel_id=1, source_target_pairs={{0,5},{1,6},{2,7},{3,8},{4,9},{5,10},{6,11},{7,12},{8,13},{9,14},{... | collective-permute-start | bytes 786440 | tf_op jit(solution)/shard_map/ppermute | solution.py:16
  47.2 15.1 %collective-permute-start.4 = (bf16[128,1024]{0,1:T(8,128)(2,1)S(1)}, bf16[128,1024]{0,1:T(8,128)(2,1)S(1)}, u32[]{:S(2)}, u32[]{:S(2)}) collective-permute-start(bf16[128,1024]{0,1:T(8,128)(2,1)S(1)} %pad_maximum_fusion.1), channel_id=1, source_target_pairs={{0,4},{1,5},{2,6},{3,7},{4,8},{5,9},{6,10},{7,11},{8,12},{9,13},{1... | collective-permute-start | bytes 786440 | tf_op jit(solution)/shard_map/ppermute | solution.py:16
  48.9 13.5 %collective-permute-start.5 = (bf16[128,1024]{0,1:T(8,128)(2,1)S(1)}, bf16[128,1024]{0,1:T(8,128)(2,1)S(1)}, u32[]{:S(2)}, u32[]{:S(2)}) collective-permute-start(bf16[128,1024]{0,1:T(8,128)(2,1)S(1)} %pad_maximum_fusion.1), channel_id=1, source_target_pairs={{0,3},{1,4},{2,5},{3,6},{4,7},{5,8},{6,9},{7,10},{8,11},{9,12},{10... | collective-permute-start | bytes 786440 | tf_op jit(solution)/shard_map/ppermute | solution.py:16
  64.0 6.9 %copy-start.4 = (bf16[1152,512]{0,1:T(8,128)(2,1)}, bf16[1152,512]{0,1:T(8,128)(2,1)S(1)}, u32[]{:S(2)}) copy-start(bf16[1152,512]{0,1:T(8,128)(2,1)S(1)} %get-tuple-element.33) | copy-start | bytes 3538948
  87.3 5.6 %copy-start.8 = (bf16[1,128,2560]{1,2,0:T(8,128)(2,1)S(1)}, bf16[1,128,2560]{1,2,0:T(8,128)(2,1)}, u32[]{:S(2)}) copy-start(bf16[1,128,2560]{1,2,0:T(8,128)(2,1)} %copy-done.7) | copy-start | bytes 1966084
  99.3 138.1 %copy-start.2 = (f32[1152,512]{1,0:T(8,128)S(1)}, f32[1152,512]{1,0:T(8,128)}, u32[]{:S(2)}) copy-start(f32[1152,512]{1,0:T(8,128)} %copy.102) | copy-start | bytes 7077892
  101.3 16.7 %collective-permute-start.8 = (f32[128,1024]{1,0:T(8,128)S(1)}, f32[128,1024]{1,0:T(8,128)S(1)}, u32[]{:S(2)}, u32[]{:S(2)}) collective-permute-start(f32[128,1024]{1,0:T(8,128)S(1)} %get-tuple-element.25), channel_id=1, source_target_pairs={{1,0},{2,1},{3,2},{4,3},{5,4},{6,5},{7,6},{8,7},{9,8},{10,9},{11,1... | collective-permute-start | bytes 1572872 | tf_op jit(solution)/shard_map/ppermute | solution.py:16
  103.3 20.1 %collective-permute-start.9 = (f32[128,1024]{1,0:T(8,128)S(1)}, f32[128,1024]{1,0:T(8,128)S(1)}, u32[]{:S(2)}, u32[]{:S(2)}) collective-permute-start(f32[128,1024]{1,0:T(8,128)S(1)} %get-tuple-element.26), channel_id=1, source_target_pairs={{2,0},{3,1},{4,2},{5,3},{6,4},{7,5},{8,6},{9,7},{10,8},{11,9},{12,... | collective-permute-start | bytes 1572872 | tf_op jit(solution)/shard_map/ppermute | solution.py:16
  105.2 29.1 %collective-permute-start.10 = (f32[128,1024]{1,0:T(8,128)S(1)}, f32[128,1024]{1,0:T(8,128)S(1)}, u32[]{:S(2)}, u32[]{:S(2)}) collective-permute-start(f32[128,1024]{1,0:T(8,128)S(1)} %get-tuple-element.27), channel_id=1, source_target_pairs={{3,0},{4,1},{5,2},{6,3},{7,4},{8,5},{9,6},{10,7},{11,8},{12,9},{13... | collective-permute-start | bytes 1572872 | tf_op jit(solution)/shard_map/ppermute | solution.py:16
  106.7 48.7 %collective-permute-start.11 = (f32[128,1024]{1,0:T(8,128)S(1)}, f32[128,1024]{1,0:T(8,128)S(1)}, u32[]{:S(2)}, u32[]{:S(2)}) collective-permute-start(f32[128,1024]{1,0:T(8,128)S(1)} %get-tuple-element.28), channel_id=1, source_target_pairs={{4,0},{5,1},{6,2},{7,3},{8,4},{9,5},{10,6},{11,7},{12,8},{13,9},{1... | collective-permute-start | bytes 1572872 | tf_op jit(solution)/shard_map/ppermute | solution.py:16
  108.0 47.4 %collective-permute-start.12 = (f32[128,1024]{1,0:T(8,128)S(1)}, f32[128,1024]{1,0:T(8,128)S(1)}, u32[]{:S(2)}, u32[]{:S(2)}) collective-permute-start(f32[128,1024]{1,0:T(8,128)S(1)} %get-tuple-element.29), channel_id=1, source_target_pairs={{5,0},{6,1},{7,2},{8,3},{9,4},{10,5},{11,6},{12,7},{13,8},{14,9},{... | collective-permute-start | bytes 1572872 | tf_op jit(solution)/shard_map/ppermute | solution.py:16
  118.0 80.9 %collective-permute-start.13 = (f32[128,1024]{1,0:T(8,128)S(1)}, f32[128,1024]{1,0:T(8,128)S(1)}, u32[]{:S(2)}, u32[]{:S(2)}) collective-permute-start(f32[128,1024]{1,0:T(8,128)S(1)} %get-tuple-element.30), channel_id=1, source_target_pairs={{6,0},{7,1},{8,2},{9,3},{10,4},{11,5},{12,6},{13,7},{14,8},{15,9},... | collective-permute-start | bytes 1572872 | tf_op jit(solution)/shard_map/ppermute | solution.py:16
  123.4 81.3 %collective-permute-start.15 = (f32[128,1024]{1,0:T(8,128)S(1)}, f32[128,1024]{1,0:T(8,128)S(1)}, u32[]{:S(2)}, u32[]{:S(2)}) collective-permute-start(f32[128,1024]{1,0:T(8,128)S(1)} %get-tuple-element.31), channel_id=1, source_target_pairs={{8,0},{9,1},{10,2},{11,3},{12,4},{13,5},{14,6},{15,7},{16,8},{17,9... | collective-permute-start | bytes 1572872 | tf_op jit(solution)/shard_map/ppermute | solution.py:16
  134.3 103.1 %collective-permute-start.14 = (f32[128,1024]{1,0:T(8,128)S(1)}, f32[128,1024]{1,0:T(8,128)S(1)}, u32[]{:S(2)}, u32[]{:S(2)}) collective-permute-start(f32[128,1024]{1,0:T(8,128)S(1)} %get-tuple-element.32), channel_id=1, source_target_pairs={{7,0},{8,1},{9,2},{10,3},{11,4},{12,5},{13,6},{14,7},{15,8},{16,9}... | collective-permute-start | bytes 1572872 | tf_op jit(solution)/shard_map/ppermute | solution.py:16
  242.2 29.1 %all-to-all-start = ((bf16[8,128,4,8,1,20]{1,3,5,4,2,0:T(8,128)(2,1)}), bf16[8,128,4,8,1,20]{1,3,5,4,2,0:T(8,128)(2,1)S(1)}, u32[]{:S(2)}, u32[]{:S(2)}) async-start(bf16[8,128,4,8,1,20]{1,3,5,4,2,0:T(8,128)(2,1)} %copy.113), calls=%async_computation | async-start | bytes 2621440 | tf_op jit(solution)/shard_map/all_to_all | solution.py:38
  304.4 89.5 %copy-start.5 = (bf16[1152,512]{0,1:T(8,128)(2,1)S(1)}, bf16[1152,512]{0,1:T(8,128)(2,1)}, u32[]{:S(2)}) copy-start(bf16[1152,512]{0,1:T(8,128)(2,1)} %copy-done.4) | copy-start | bytes 3538948
  392.5 6.4 %copy-start.6 = (bf16[4,128,5,128]{3,1,2,0:T(8,128)(2,1)S(1)}, bf16[4,128,5,128]{3,1,2,0:T(8,128)(2,1)}, u32[]{:S(2)}) copy-start(bf16[4,128,5,128]{3,1,2,0:T(8,128)(2,1)} %get-tuple-element.40) | copy-start | bytes 1966084
  392.5 22.9 %collective-permute-start.21 = (f32[4,1024]{1,0:T(4,128)S(1)}, f32[4,1024]{1,0:T(4,128)S(1)}, u32[]{:S(2)}, u32[]{:S(2)}) collective-permute-start(f32[4,1024]{1,0:T(4,128)S(1)} %slice.72), channel_id=1, source_target_pairs={{0,48},{8,56},{16,64},{24,72},{32,80},{40,88},{48,96},{56,104},{64... | collective-permute-start | bytes 49160
  397.8 21.0 %copy-start.9 = (bf16[128,1024]{1,0:T(8,128)(2,1)S(1)}, bf16[128,1024]{1,0:T(8,128)(2,1)}, u32[]{:S(2)}) copy-start(bf16[128,1024]{1,0:T(8,128)(2,1)} %fusion.32) | copy-start | bytes 786436
  400.0 19.5 %collective-permute-start.20 = (f32[24,1024]{1,0:T(8,128)S(1)}, f32[24,1024]{1,0:T(8,128)S(1)}, u32[]{:S(2)}, u32[]{:S(2)}) collective-permute-start(f32[24,1024]{1,0:T(8,128)S(1)} %fusion), channel_id=1, source_target_pairs={{0,40},{8,48},{16,56},{24,64},{32,72},{40,80},{48,88},{56,96},{64,... | collective-permute-start | bytes 294920
  401.3 18.2 %collective-permute-start.19 = (f32[24,1024]{1,0:T(8,128)S(1)}, f32[24,1024]{1,0:T(8,128)S(1)}, u32[]{:S(2)}, u32[]{:S(2)}) collective-permute-start(f32[24,1024]{1,0:T(8,128)S(1)} %fusion), channel_id=1, source_target_pairs={{0,32},{8,40},{16,48},{24,56},{32,64},{40,72},{48,80},{56,88},{64,... | collective-permute-start | bytes 294920
  406.5 13.1 %collective-permute-start.18 = (f32[24,1024]{1,0:T(8,128)S(1)}, f32[24,1024]{1,0:T(8,128)S(1)}, u32[]{:S(2)}, u32[]{:S(2)}) collective-permute-start(f32[24,1024]{1,0:T(8,128)S(1)} %fusion), channel_id=1, source_target_pairs={{0,24},{8,32},{16,40},{24,48},{32,56},{40,64},{48,72},{56,80},{64,... | collective-permute-start | bytes 294920
  411.6 10.5 %collective-permute-start.17 = (f32[24,1024]{1,0:T(8,128)S(1)}, f32[24,1024]{1,0:T(8,128)S(1)}, u32[]{:S(2)}, u32[]{:S(2)}) collective-permute-start(f32[24,1024]{1,0:T(8,128)S(1)} %fusion), channel_id=1, source_target_pairs={{0,16},{8,24},{16,32},{24,40},{32,48},{40,56},{48,64},{56,72},{64,... | collective-permute-start | bytes 294920
  415.4 8.0 %collective-permute-start.16 = (f32[24,1024]{1,0:T(8,128)S(1)}, f32[24,1024]{1,0:T(8,128)S(1)}, u32[]{:S(2)}, u32[]{:S(2)}) collective-permute-start(f32[24,1024]{1,0:T(8,128)S(1)} %fusion), channel_id=1, source_target_pairs={{0,8},{8,16},{16,24},{24,32},{32,40},{40,48},{48,56},{56,64},{64,7... | collective-permute-start | bytes 294920
  (5 other events, 17.8 us)
Sparse Core Ops, SparseCore 0:
  238.6 61.0 all-gather.1
